TPU v7x, 32 devices: a whole 2x2x4 slice. The times are simulated.
32 devices in a mesh: scene: 4 (over y, core), frame: 8 (over z, x).
Axes of the slice: x: 2, y: 2, z: 4, core: 2. Of those that a mesh axis runs over, the one named last changes fastest.
Arguments:
- occupancy: bfloat16 [4, 32, 64, 2048], P('scene', 'frame'), may hold values from -6 to 6
- scene_lengths: int32 [4], P('scene'), may hold values from 8 to 32, as said below
- conv1_weight: bfloat16 [128, 1728], replicated, may hold values from -0.15625 to 0.15625
- conv2_weight: bfloat16 [256, 3456], replicated, may hold values from -0.109375 to 0.109375
- temporal_weight: bfloat16 [3, 256, 256], replicated, may hold values from -0.21875 to 0.21875
- query_weight: bfloat16 [256, 256], replicated
- key_weight: bfloat16 [256, 256], replicated
- value_weight: bfloat16 [256, 256], replicated, may hold values from -0.375 to 0.375
- out_weight: bfloat16 [256, 256], replicated, may hold values from -0.375 to 0.375
Outputs:
- encoded: bfloat16 [4, 32, 256, 512], P('scene', 'frame')
- kl_loss: float32 [], replicated
Inputs may be any that keep to these rules, and one draw needn't show every extreme that they name: `scene_lengths`: non-decreasing along the scenes; the first scene has exactly 8 frames with data and the last exactly 32.
All inputs are finite; a program needn't handle non-finite values.
Results may differ from a plain program's by a relative error of at most 0.011.
Values may be sent and summed in bfloat16 or wider, within the bound.
No kernel may reach another device: no remote copies, remote signals or barrier semaphores. Data moves between devices by JAX's collectives and lax.ppermute only.
A program may use at most 192 MiB of HBM per device.

v0:
```python
import jax
import jax.numpy as jnp
from jax import lax
from jax.sharding import PartitionSpec as P

CIN = 64
C1 = 128
C2 = 256
HEADS = 4
HD = 64
HI = 16
ZD = 8
CELLS = 512
NORM_EPS = 1e-06


def spatial_conv(voxels, weight, channels_in, stride):
    channels_out = weight.shape[0]
    kernel = weight.reshape(channels_out, channels_in, 3, 3, 3)
    return lax.conv_general_dilated(
        voxels,
        kernel,
        (stride, stride, 1),
        ((1, 1), (1, 1), (1, 1)),
        dimension_numbers=("NCDHW", "OIDHW", "NCDHW"),
        preferred_element_type=jnp.float32,
    )


def mix_channels(weight, maps):
    return jnp.einsum("oc,fcn->fon", weight, maps, preferred_element_type=jnp.float32)


def temporal_block(padded, second_maps, temporal_weight):
    count_frames = second_maps.shape[0]
    temporal_sum = mix_channels(temporal_weight[0], padded[0:count_frames])
    for tap in range(1, 3):
        temporal_sum = temporal_sum + mix_channels(
            temporal_weight[tap], padded[tap : tap + count_frames]
        )
    residual_maps = (second_maps.astype(jnp.float32) + jax.nn.silu(temporal_sum)).astype(
        jnp.bfloat16
    )
    return residual_maps.astype(jnp.float32)


def project_rows(residual_f, query_weight, key_weight, value_weight):
    count_frames = residual_f.shape[0]
    count_cells = residual_f.shape[2]
    normed = (
        residual_f * lax.rsqrt(jnp.mean(residual_f * residual_f, axis=1, keepdims=True) + NORM_EPS)
    ).astype(jnp.bfloat16)
    queries = (
        mix_channels(query_weight, normed)
        .astype(jnp.bfloat16)
        .reshape(count_frames, HEADS, HD, count_cells)
    )
    key_rows = (
        mix_channels(key_weight, normed)
        .astype(jnp.bfloat16)
        .reshape(count_frames, HEADS, HD, count_cells)
    )
    value_rows = (
        mix_channels(value_weight, normed)
        .astype(jnp.bfloat16)
        .reshape(count_frames, HEADS, HD, count_cells)
    )
    return (queries, key_rows, value_rows)


def finish_rows(residual_f, attended, out_weight, valid_rows):
    count_frames = residual_f.shape[0]
    count_cells = residual_f.shape[2]
    out_full = residual_f + mix_channels(
        out_weight, attended.reshape(count_frames, C2, count_cells)
    )
    return (out_full * valid_rows[:, None, None]).astype(jnp.bfloat16)


def attend_whole(queries, key_rows, value_rows, length):
    scores = jnp.einsum(
        "qhdc,khdc->qkhc", queries, key_rows, preferred_element_type=jnp.float32
    ) * HD ** (-0.5)
    key_mask = (jnp.arange(key_rows.shape[0]) < length)[None, :, None, None]
    scores = jnp.where(key_mask, scores, -1e30)
    row_max = jnp.max(scores, axis=1, keepdims=True)
    raw_weights = jnp.where(key_mask, jnp.exp(scores - row_max), 0.0)
    row_total = jnp.sum(raw_weights, axis=1)
    weighted = jnp.einsum(
        "qkhc,khdc->qhdc",
        raw_weights.astype(jnp.bfloat16),
        value_rows,
        preferred_element_type=jnp.float32,
    )
    return (weighted / row_total[:, :, None, :]).astype(jnp.bfloat16)


def shards(
    occupancy,
    scene_lengths,
    conv1_weight,
    conv2_weight,
    temporal_weight,
    query_weight,
    key_weight,
    value_weight,
    out_weight,
):
    f_dev = occupancy.shape[1]
    length = scene_lengths[0]
    first_frame = lax.axis_index("frame") * f_dev
    frame_ids = first_frame + jnp.arange(f_dev, dtype=jnp.int32)
    valid_rows = (frame_ids < length).astype(jnp.float32)
    voxels = occupancy[0].reshape(f_dev, CIN, HI, HI, ZD)
    first_maps = jax.nn.silu(spatial_conv(voxels, conv1_weight, CIN, 2)).astype(jnp.bfloat16)
    second_full = jax.nn.silu(spatial_conv(first_maps, conv2_weight, C1, 1))
    second_maps = (second_full.reshape(f_dev, C2, CELLS) * valid_rows[:, None, None]).astype(
        jnp.bfloat16
    )
    cell_maps = lax.all_to_all(second_maps, "frame", split_axis=2, concat_axis=0, tiled=True)
    frames_all = cell_maps.shape[0]
    padded_all = jnp.pad(cell_maps, ((1, 1), (0, 0), (0, 0)))
    residual_cols = temporal_block(padded_all, cell_maps, temporal_weight)
    queries, key_rows, value_rows = project_rows(
        residual_cols, query_weight, key_weight, value_weight
    )
    attended_cols = attend_whole(queries, key_rows, value_rows, length)
    valid_all = (jnp.arange(frames_all, dtype=jnp.int32) < length).astype(jnp.float32)
    encoded_cols = finish_rows(residual_cols, attended_cols, out_weight, valid_all)
    encoded = lax.all_to_all(encoded_cols, "frame", split_axis=0, concat_axis=2, tiled=True)
    squares = jnp.sum(jnp.square(encoded.astype(jnp.float32)))
    grand_total = lax.psum(squares, ("scene", "frame"))
    slot_count = float(lax.axis_size("scene") * lax.axis_size("frame") * f_dev * CELLS * C2)
    kl_loss = 0.5 * grand_total / slot_count
    return (encoded[None], kl_loss)


def solution(mesh):
    placed = (P("scene", "frame", None, None), P("scene"), P(), P(), P(), P(), P(), P(), P())
    return jax.shard_map(
        shards,
        mesh=mesh,
        in_specs=placed,
        out_specs=(P("scene", "frame", None, None), P()),
        check_vma=False,
    )
```

profile of v0, /device:TPU:0, one launch (start us, length us, event | category | flops | bytes accessed | tf_op | source)
XLA Modules:
  0.0 175.9 jit_solution(6949162272916972994)
XLA Ops:
  1.3 2.6 %copy.50 = bf16[256,3456]{0,1:T(8,128)(2,1)S(1)} copy(bf16[256,3456]{1,0:T(8,128)(2,1)} %param.12) | data formatting | bytes 3538944 | tf_op args[3]
  4.0 2.9 %reshape.52 = bf16[256,128,3,3,3]{0,4,3,2,1:T(4,128)(2,1)} reshape(bf16[256,3456]{0,1:T(8,128)(2,1)S(1)} %copy.50) | data formatting | bytes 3538944 | tf_op jit(solution)/shard_map/reshape | solution.py:19
  6.9 1.1 copy.47
  7.9 1.5 reshape.51
  9.4 5.0 %fusion.32 = bf16[4,128,8,8,8]{1,0,4,3,2:T(4,128)(2,1)S(1)} fusion(bf16[4,64,16,16,8]{1,4,3,2,0:T(8,128)(2,1)S(1)} %bitcast.108, bf16[128,64,3,3,3]{0,4,3,2,1:T(4,128)(2,1)S(1)} %reshape.51), kind=kOutput, calls=%fused_computation.44 | convolution fusion | flops 764018688 | bytes 2015232 | tf_op jit(solution)/shard_map/conv_general_dilated | solution.py:20
  14.4 6.6 %divide_multiply_fusion = f32[4,256,8,8,8]{1,0,4,3,2:T(4,128)S(1)} fusion(bf16[4,128,8,8,8]{1,0,4,3,2:T(4,128)(2,1)S(1)} %fusion.32, bf16[256,128,3,3,3]{0,4,3,2,1:T(4,128)(2,1)S(1)} %copy-done.1), kind=kOutput, calls=%fused_computation.6 | convolution fusion | flops 2793406464 | bytes 4390912 | tf_op jit(solution)/shard_map/conv_general_dilated | solution.py:20
  21.1 1.5 fusion.13
  22.6 7.4 %all-to-all-start = ((bf16[4,256,512]{1,0,2:T(4,128)(2,1)}), bf16[4,256,512]{1,0,2:T(4,128)(2,1)S(1)}, u32[]{:S(2)}, u32[]{:S(2)}) async-start(bf16[4,256,512]{1,0,2:T(4,128)(2,1)} %fusion.13), calls=%async_computation | async-start | bytes 2097152 | tf_op jit(solution)/shard_map/all_to_all | solution.py:120
  30.0 25.8 %all-to-all-done = bf16[4,256,512]{1,0,2:T(4,128)(2,1)S(1)} async-done(((bf16[4,256,512]{1,0,2:T(4,128)(2,1)}), bf16[4,256,512]{1,0,2:T(4,128)(2,1)S(1)}, u32[]{:S(2)}, u32[]{:S(2)}) %all-to-all-start) | async-done | bytes 1048608 | tf_op jit(solution)/shard_map/all_to_all | solution.py:120
  55.8 0.2 copy.52
  56.0 0.5 fusion.45
  56.4 0.5 fusion.47
  56.9 1.2 fusion.2
  58.1 1.5 fusion.26
  59.6 3.4 %reshape.55 = bf16[32,4,64,64]{2,1,3,0:T(4,128)(2,1)S(1)} reshape(bf16[32,256,64]{1,2,0:T(8,128)(2,1)} %fusion.26) | data formatting | bytes 2097152 | tf_op jit(solution)/shard_map/reshape | solution.py:61
  62.9 1.5 fusion.27
  64.4 4.4 %reshape.56 = bf16[32,4,64,64]{2,1,3,0:T(4,128)(2,1)} reshape(bf16[32,256,64]{1,2,0:T(8,128)(2,1)} %fusion.27) | data formatting | bytes 2097152 | tf_op jit(solution)/shard_map/reshape | solution.py:56
  68.8 8.1 %fusion.15 = f32[4,64,32,32]{3,2,1,0:T(8,128)} fusion(bf16[32,4,64,64]{2,1,3,0:T(4,128)(2,1)} %reshape.56, bf16[32,4,64,64]{2,1,3,0:T(4,128)(2,1)S(1)} %reshape.55), kind=kOutput, calls=%fused_computation.25 | convolution fusion | flops 33554432 | bytes 3145728 | tf_op jit(solution)/shard_map/qhdc,khdc->qkhc/dot_general | solution.py:81
  77.0 4.6 %copy.55 = f32[4,64,32,32]{1,2,0,3:T(8,128)S(1)} copy(f32[4,64,32,32]{3,2,1,0:T(8,128)} %fusion.15) | data formatting | bytes 2097152 | tf_op jit(solution)/shard_map/qhdc,khdc->qkhc/dot_general | solution.py:81
  81.6 1.9 %fusion.55 = (f32[32,4,64]{2,1,0:T(4,128)S(1)}, bf16[32,32,4,64]{3,1,2,0:T(8,128)(2,1)}) fusion(f32[4,64,32,32]{1,2,0,3:T(8,128)S(1)} %copy.55, pred[32]{0:T(512)(128)(4,1)S(1)} %get-tuple-element.13), kind=kOutput, calls=%fused_computation.65 | output fusion | flops 2097183 | bytes 1605664 | tf_op jit(solution)/shard_map/sub | solution.py:87
  83.5 4.8 %copy.57 = bf16[32,32,4,64]{1,0,3,2:T(8,128)(2,1)} copy(bf16[32,32,4,64]{3,1,2,0:T(8,128)(2,1)} %get-tuple-element.9) | data formatting | bytes 1048576 | tf_op jit(solution)/shard_map/convert_element_type | solution.py:91
  88.4 0.5 fusion.25
  88.9 1.8 %reshape.54 = bf16[32,4,64,64]{2,1,3,0:T(4,128)(2,1)} reshape(bf16[32,256,64]{1,2,0:T(8,128)(2,1)S(1)} %fusion.25) | data formatting | bytes 2097152 | tf_op jit(solution)/shard_map/reshape | solution.py:66
  90.7 7.1 %fusion.1 = bf16[32,4,64,64]{2,0,3,1:T(8,128)(2,1)S(1)} fusion(bf16[32,32,4,64]{1,0,3,2:T(8,128)(2,1)} %copy.57, bf16[32,4,64,64]{2,1,3,0:T(4,128)(2,1)} %reshape.54, f32[32,4,64]{0,2,1:T(8,128)S(1)} %copy.58), kind=kOutput, calls=%fused_computation.2 | convolution fusion | flops 34603008 | bytes 2654208 | tf_op jit(solution)/shard_map/qkhc,khdc->qhdc/dot_general | solution.py:89
  97.8 1.6 copy.59
  99.4 2.2 %reshape.57 = bf16[32,256,64]{1,2,0:T(8,128)(2,1)} reshape(bf16[32,4,64,64]{2,1,3,0:T(4,128)(2,1)S(1)} %copy.59) | data formatting | bytes 2097152 | tf_op jit(solution)/shard_map/reshape | solution.py:75
  101.6 1.7 fusion.5
  103.3 29.3 %all_to_all.33 = bf16[32,256,64]{1,2,0:T(8,128)(2,1)S(1)} all-to-all(bf16[32,256,64]{1,2,0:T(8,128)(2,1)S(1)} %fusion.5), channel_id=1, replica_groups=mesh['scene'=4,'frame'=8] {'frame'}, dimensions={0} | all-to-all | bytes 2097152 | tf_op jit(solution)/shard_map/all_to_all | solution.py:130
  132.6 0.1 copy.60
  132.7 1.1 multiply_reduce_fusion
  133.8 1.3 copy.61
  135.1 39.0 %psum.7 = f32[]{:T(128)} all-reduce(f32[]{:T(128)} %multiply_reduce_fusion), channel_id=1, replica_groups=mesh['scene'=4,'frame'=8] {'scene','frame'}, use_global_device_ids=true, to_apply=%region_4.5 | all-reduce | flops 1 | bytes 8 | tf_op jit(solution)/shard_map/psum | solution.py:132
  (18 shorter events, 0.2 us)
Async XLA Ops:
  0.6 57.5 %copy-start = (bf16[256,256]{1,0:T(8,128)(2,1)S(1)}, bf16[256,256]{1,0:T(8,128)(2,1)}, u32[]{:S(2)}) copy-start(bf16[256,256]{1,0:T(8,128)(2,1)} %param.15) | copy-start | bytes 393220
  4.0 2.9 %copy-start.2 = (bf16[1,4,64,2048]{3,2,1,0:T(8,128)(2,1)S(1)}, bf16[1,4,64,2048]{3,2,1,0:T(8,128)(2,1)}, u32[]{:S(2)}) copy-start(bf16[1,4,64,2048]{3,2,1,0:T(8,128)(2,1)} %param.9) | copy-start | bytes 3145732
  9.4 5.0 %copy-start.1 = (bf16[256,128,3,3,3]{0,4,3,2,1:T(4,128)(2,1)S(1)}, bf16[256,128,3,3,3]{0,4,3,2,1:T(4,128)(2,1)}, u32[]{:S(2)}) copy-start(bf16[256,128,3,3,3]{0,4,3,2,1:T(4,128)(2,1)} %reshape.52) | copy-start | bytes 5308420
  22.6 33.4 %copy-start.3 = (bf16[3,256,256]{2,1,0:T(8,128)(2,1)S(1)}, bf16[3,256,256]{2,1,0:T(8,128)(2,1)}, u32[]{:S(2)}) copy-start(bf16[3,256,256]{2,1,0:T(8,128)(2,1)} %param.13) | copy-start | bytes 1179652
  22.6 33.2 %all-to-all-start = ((bf16[4,256,512]{1,0,2:T(4,128)(2,1)}), bf16[4,256,512]{1,0,2:T(4,128)(2,1)S(1)}, u32[]{:S(2)}, u32[]{:S(2)}) async-start(bf16[4,256,512]{1,0,2:T(4,128)(2,1)} %fusion.13), calls=%async_computation | async-start | bytes 2097152 | tf_op jit(solution)/shard_map/all_to_all | solution.py:120
  59.6 3.4 %copy-start.4 = (bf16[256,256]{1,0:T(8,128)(2,1)S(1)}, bf16[256,256]{1,0:T(8,128)(2,1)}, u32[]{:S(2)}) copy-start(bf16[256,256]{1,0:T(8,128)(2,1)} %param.14) | copy-start | bytes 393220
  83.5 4.9 %copy-start.5 = (bf16[256,256]{1,0:T(8,128)(2,1)S(1)}, bf16[256,256]{1,0:T(8,128)(2,1)}, u32[]{:S(2)}) copy-start(bf16[256,256]{1,0:T(8,128)(2,1)} %param.16) | copy-start | bytes 393220
  99.4 2.2 %copy-start.6 = (bf16[256,256]{1,0:T(8,128)(2,1)S(1)}, bf16[256,256]{1,0:T(8,128)(2,1)}, u32[]{:S(2)}) copy-start(bf16[256,256]{1,0:T(8,128)(2,1)} %param.17) | copy-start | bytes 393220
where the time goes:
time: 176 us
  blocking collectives  68.2 us (39%)
  matrix products  34 us (19%)
  local copies, waits for them, and re-layouts  32.5 us (18%)
  waiting for transfers between devices  25.8 us (15%)
  starting transfers between devices  7.41 us (4%)
  other arithmetic  4.62 us (3%)
  between operations  3.32 us (2%)
    psum x1, blocking collectives, shards(): grand_total = lax.psum(squares, ('scene', 'frame'))  39 us
    all_to_all x1, blocking collectives, shards(): lax.all_to_all(encoded_cols, 'frame', split_axis=0, concat_axis=2, tiled=...  29.3 us
    all_to_all x1, waiting for transfers between devices, shards(): lax.all_to_all(second_maps, 'frame', split_axis=2, concat_axis=0, tiled=T...  25.8 us
    conv_general_dilated x2, matrix products, spatial_conv(): lax.conv_general_dilated(voxels, kernel, (stride, stride, 1), ((1, 1), (1...  11.6 us
    dot_general x1, matrix products, attend_whole(): jnp.einsum('qhdc,khdc->qkhc', queries, key_rows, preferred_element_type=j...  8.13 us
    all_to_all x1, starting transfers between devices, shards(): lax.all_to_all(second_maps, 'frame', split_axis=2, concat_axis=0, tiled=T...  7.41 us
    dot_general x7, matrix products, mix_channels(): jnp.einsum('oc,fcn->fon', weight, maps, preferred_element_type=jnp.float32)  7.2 us
    dot_general x1, matrix products, attend_whole(): jnp.einsum('qkhc,khdc->qhdc', raw_weights.astype(jnp.bfloat16), value_row...  7.06 us
  transfers between devices with their start and end apart: 1, of which 1 were waited for; matrix products, arithmetic and copies ran while one was open for 0% of the time, Pallas kernels for 0%

commit v1 on v0

--- a/solution.py
+++ b/solution.py
@@ -117,7 +117,15 @@
     second_maps = (second_full.reshape(f_dev, C2, CELLS) * valid_rows[:, None, None]).astype(
         jnp.bfloat16
     )
-    cell_maps = lax.all_to_all(second_maps, "frame", split_axis=2, concat_axis=0, tiled=True)
+    ways, here = (lax.axis_size("frame"), lax.axis_index("frame"))
+    width = second_maps.shape[2] // ways
+    turned = jnp.roll(second_maps, -here * width, axis=2)
+    got = [lax.slice_in_dim(turned, 0, width, axis=2)]
+    for far in range(1, ways):
+        sent = lax.slice_in_dim(turned, far * width, (far + 1) * width, axis=2)
+        got.append(lax.ppermute(sent, "frame", [(d, (d + far) % ways) for d in range(ways)]))
+    line = jnp.concatenate(got[::-1], axis=0)
+    cell_maps = jnp.roll(line, (here + 1) * got[0].shape[0], axis=0)
     frames_all = cell_maps.shape[0]
     padded_all = jnp.pad(cell_maps, ((1, 1), (0, 0), (0, 0)))
     residual_cols = temporal_block(padded_all, cell_maps, temporal_weight)

time: 176 us -> 174 us (0.989)
  waiting for transfers between devices: 25.8 us -> 18.9 us
  starting transfers between devices: 7.41 us -> 11 us
    all_to_all x1 -> x0, waiting for transfers between devices: 25.8 us -> none  [shards(): lax.all_to_all(second_maps, 'frame', split_axis=2, concat_axis=0, tiled=T...]
    ppermute x0 -> x7, waiting for transfers between devices: none -> 18.9 us  [shards(): lax.ppermute(sent, 'frame', [(d, (d + far) % ways) for d in range(ways)])]
    ppermute x0 -> x7, starting transfers between devices: none -> 11 us  [shards(): lax.ppermute(sent, 'frame', [(d, (d + far) % ways) for d in range(ways)])]
    all_to_all x1 -> x0, starting transfers between devices: 7.41 us -> none  [shards(): lax.all_to_all(second_maps, 'frame', split_axis=2, concat_axis=0, tiled=T...]
    unnamed x17 -> x32, local copies, waits for them, and re-layouts: 5.04 us -> 6.93 us
  transfers between devices with their start and end apart: 1 -> 7, of which waited for: 1 -> 5; matrix products, arithmetic and copies ran while one was open for 0% -> 0% of each run, Pallas kernels for 0% -> 0%
where the time goes in v1:
time: 174 us
  blocking collectives  68.1 us (39%)
  matrix products  34.9 us (20%)
  local copies, waits for them, and re-layouts  32.8 us (19%)
  waiting for transfers between devices  18.9 us (11%)
  starting transfers between devices  11 us (6%)
  other arithmetic  4.69 us (3%)
  between operations  3.43 us (2%)
    psum x1, blocking collectives, shards(): grand_total = lax.psum(squares, ('scene', 'frame'))  39 us
    all_to_all x1, blocking collectives, shards(): lax.all_to_all(encoded_cols, 'frame', split_axis=0, concat_axis=2, tiled=...  29.1 us
    ppermute x7, waiting for transfers between devices, shards(): lax.ppermute(sent, 'frame', [(d, (d + far) % ways) for d in range(ways)])  18.9 us
    conv_general_dilated x2, matrix products, spatial_conv(): lax.conv_general_dilated(voxels, kernel, (stride, stride, 1), ((1, 1), (1...  12.5 us
    ppermute x7, starting transfers between devices, shards(): lax.ppermute(sent, 'frame', [(d, (d + far) % ways) for d in range(ways)])  11 us
    dot_general x1, matrix products, attend_whole(): jnp.einsum('qhdc,khdc->qkhc', queries, key_rows, preferred_element_type=j...  8.14 us
    dot_general x7, matrix products, mix_channels(): jnp.einsum('oc,fcn->fon', weight, maps, preferred_element_type=jnp.float32)  7.21 us
    dot_general x1, matrix products, attend_whole(): jnp.einsum('qkhc,khdc->qhdc', raw_weights.astype(jnp.bfloat16), value_row...  7.07 us
  transfers between devices with their start and end apart: 7, of which 5 were waited for; matrix products, arithmetic and copies ran while one was open for 0% of the time, Pallas kernels for 0%

profile of v1, /device:TPU:0, one launch (start us, length us, event | category | flops | bytes accessed | tf_op | source)
XLA Modules:
  0.0 173.8 jit_solution(8046543520992738304)
XLA Ops:
  0.7 2.8 %copy.47 = bf16[1,4,64,2048]{2,3,1,0:T(8,128)(2,1)} copy(bf16[1,4,64,2048]{3,2,1,0:T(8,128)(2,1)} %param.9) | data formatting | bytes 2097152 | tf_op args[0]
  3.7 2.6 %copy.50 = bf16[256,3456]{0,1:T(8,128)(2,1)S(1)} copy(bf16[256,3456]{1,0:T(8,128)(2,1)} %param.12) | data formatting | bytes 3538944 | tf_op args[3]
  6.3 2.9 %reshape.52 = bf16[256,128,3,3,3]{0,4,3,2,1:T(4,128)(2,1)} reshape(bf16[256,3456]{0,1:T(8,128)(2,1)S(1)} %copy.50) | data formatting | bytes 3538944 | tf_op jit(solution)/shard_map/reshape | solution.py:19
  9.9 5.9 %fusion.33 = bf16[4,128,8,8,8]{1,0,4,3,2:T(4,128)(2,1)S(1)} fusion(bf16[4,64,16,16,8]{1,4,3,2,0:T(8,128)(2,1)} %bitcast.94, bf16[128,64,3,3,3]{0,4,3,2,1:T(4,128)(2,1)S(1)} %reshape.51), kind=kOutput, calls=%fused_computation.47 | convolution fusion | flops 764018688 | bytes 2015232 | tf_op jit(solution)/shard_map/conv_general_dilated | solution.py:20
  15.8 6.6 %divide_multiply_fusion = f32[4,256,8,8,8]{1,0,4,3,2:T(4,128)S(1)} fusion(bf16[4,128,8,8,8]{1,0,4,3,2:T(4,128)(2,1)S(1)} %fusion.33, bf16[256,128,3,3,3]{0,4,3,2,1:T(4,128)(2,1)S(1)} %copy-done.1), kind=kOutput, calls=%fused_computation.6 | convolution fusion | flops 2793406464 | bytes 4390912 | tf_op jit(solution)/shard_map/conv_general_dilated | solution.py:20
  22.4 0.6 fusion.17
  23.0 1.0 fusion.30
  24.1 6.1 %collective-permute-start = (bf16[4,256,64]{1,2,0:T(8,128)(2,1)S(1)}, bf16[4,256,64]{1,2,0:T(8,128)(2,1)S(1)}, u32[]{:S(2)}, u32[]{:S(2)}) collective-permute-start(bf16[4,256,64]{1,2,0:T(8,128)(2,1)S(1)} %get-tuple-element.16), channel_id=1, source_target_pairs={{0,7},{1,0},{2,1},{3,2},{4,3},{5,4},{6,5},{7,6},{8,15},{9,8},{10,9... | collective-permute-start | bytes 393224 | tf_op jit(solution)/shard_map/ppermute | solution.py:126
  30.6 3.0 %collective-permute-start.3 = (bf16[4,256,64]{1,2,0:T(8,128)(2,1)S(1)}, bf16[4,256,64]{1,2,0:T(8,128)(2,1)S(1)}, u32[]{:S(2)}, u32[]{:S(2)}) collective-permute-start(bf16[4,256,64]{1,2,0:T(8,128)(2,1)S(1)} %get-tuple-element.13), channel_id=1, source_target_pairs={{0,4},{1,5},{2,6},{3,7},{4,0},{5,1},{6,2},{7,3},{8,12},{9,13},{10,... | collective-permute-start | bytes 393224 | tf_op jit(solution)/shard_map/ppermute | solution.py:126
  34.1 1.4 collective-permute-start.5
  35.5 1.4 collective-permute-done.1
  37.0 2.8 %collective-permute-done.2 = bf16[4,256,64]{1,2,0:T(8,128)(2,1)S(1)} collective-permute-done((bf16[4,256,64]{1,2,0:T(8,128)(2,1)S(1)}, bf16[4,256,64]{1,2,0:T(8,128)(2,1)S(1)}, u32[]{:S(2)}, u32[]{:S(2)}) %collective-permute-start.2) | collective-permute-done | bytes 131104 | tf_op jit(solution)/shard_map/ppermute | solution.py:126
  39.8 12.7 %collective-permute-done.3 = bf16[4,256,64]{1,2,0:T(8,128)(2,1)S(1)} collective-permute-done((bf16[4,256,64]{1,2,0:T(8,128)(2,1)S(1)}, bf16[4,256,64]{1,2,0:T(8,128)(2,1)S(1)}, u32[]{:S(2)}, u32[]{:S(2)}) %collective-permute-start.3) | collective-permute-done | bytes 131104 | tf_op jit(solution)/shard_map/ppermute | solution.py:126
  52.5 1.6 collective-permute-done.4
  55.3 1.1 fusion.2
  56.5 1.5 fusion.27
  57.9 3.4 %reshape.56 = bf16[32,4,64,64]{2,1,3,0:T(4,128)(2,1)S(1)} reshape(bf16[32,256,64]{1,2,0:T(8,128)(2,1)} %fusion.27) | data formatting | bytes 2097152 | tf_op jit(solution)/shard_map/reshape | solution.py:56
  61.3 1.5 fusion.26
  62.8 4.4 %reshape.55 = bf16[32,4,64,64]{2,1,3,0:T(4,128)(2,1)} reshape(bf16[32,256,64]{1,2,0:T(8,128)(2,1)} %fusion.26) | data formatting | bytes 2097152 | tf_op jit(solution)/shard_map/reshape | solution.py:61
  67.2 8.1 %fusion.14 = f32[4,64,32,32]{3,2,1,0:T(8,128)} fusion(bf16[32,4,64,64]{2,1,3,0:T(4,128)(2,1)S(1)} %reshape.56, bf16[32,4,64,64]{2,1,3,0:T(4,128)(2,1)} %reshape.55), kind=kOutput, calls=%fused_computation.25 | convolution fusion | flops 33554432 | bytes 3145728 | tf_op jit(solution)/shard_map/qhdc,khdc->qkhc/dot_general | solution.py:81
  75.3 4.4 %copy.55 = f32[4,64,32,32]{1,2,0,3:T(8,128)S(1)} copy(f32[4,64,32,32]{3,2,1,0:T(8,128)} %fusion.14) | data formatting | bytes 2097152 | tf_op jit(solution)/shard_map/qhdc,khdc->qkhc/dot_general | solution.py:81
  79.7 1.9 %fusion.65 = (f32[32,4,64]{2,1,0:T(4,128)S(1)}, bf16[32,32,4,64]{3,1,2,0:T(8,128)(2,1)}) fusion(f32[4,64,32,32]{1,2,0,3:T(8,128)S(1)} %copy.55, pred[32]{0:T(512)(128)(4,1)S(1)} %get-tuple-element.20), kind=kOutput, calls=%fused_computation.91 | output fusion | flops 2097183 | bytes 1605664 | tf_op jit(solution)/shard_map/sub | solution.py:87
  81.6 4.8 %copy.57 = bf16[32,32,4,64]{1,0,3,2:T(8,128)(2,1)} copy(bf16[32,32,4,64]{3,1,2,0:T(8,128)(2,1)} %get-tuple-element.9) | data formatting | bytes 1048576 | tf_op jit(solution)/shard_map/convert_element_type | solution.py:91
  86.9 1.8 %reshape.54 = bf16[32,4,64,64]{2,1,3,0:T(4,128)(2,1)} reshape(bf16[32,256,64]{1,2,0:T(8,128)(2,1)S(1)} %fusion.25) | data formatting | bytes 2097152 | tf_op jit(solution)/shard_map/reshape | solution.py:66
  88.8 7.1 %fusion.1 = bf16[32,4,64,64]{2,0,3,1:T(8,128)(2,1)S(1)} fusion(bf16[32,32,4,64]{1,0,3,2:T(8,128)(2,1)} %copy.57, bf16[32,4,64,64]{2,1,3,0:T(4,128)(2,1)} %reshape.54, f32[32,4,64]{0,2,1:T(8,128)S(1)} %copy.58), kind=kOutput, calls=%fused_computation.2 | convolution fusion | flops 34603008 | bytes 2654208 | tf_op jit(solution)/shard_map/qkhc,khdc->qhdc/dot_general | solution.py:89
  95.9 1.6 copy.59
  97.6 2.2 %reshape.57 = bf16[32,256,64]{1,2,0:T(8,128)(2,1)} reshape(bf16[32,4,64,64]{2,1,3,0:T(4,128)(2,1)S(1)} %copy.59) | data formatting | bytes 2097152 | tf_op jit(solution)/shard_map/reshape | solution.py:75
  99.7 1.7 fusion.5
  101.4 29.1 %all_to_all.15 = bf16[32,256,64]{1,2,0:T(8,128)(2,1)S(1)} all-to-all(bf16[32,256,64]{1,2,0:T(8,128)(2,1)S(1)} %fusion.5), channel_id=1, replica_groups=mesh['scene'=4,'frame'=8] {'frame'}, dimensions={0} | all-to-all | bytes 2097152 | tf_op jit(solution)/shard_map/all_to_all | solution.py:138
  130.7 1.1 multiply_reduce_fusion
  131.8 1.3 copy.61
  133.1 39.0 %psum.7 = f32[]{:T(128)} all-reduce(f32[]{:T(128)} %multiply_reduce_fusion), channel_id=1, replica_groups=mesh['scene'=4,'frame'=8] {'scene','frame'}, use_global_device_ids=true, to_apply=%region_4.5 | all-reduce | flops 1 | bytes 8 | tf_op jit(solution)/shard_map/psum | solution.py:140
  (47 shorter events, 3.1 us)
Async XLA Ops:
  0.6 55.8 %copy-start = (bf16[256,256]{1,0:T(8,128)(2,1)S(1)}, bf16[256,256]{1,0:T(8,128)(2,1)}, u32[]{:S(2)}) copy-start(bf16[256,256]{1,0:T(8,128)(2,1)} %param.14) | copy-start | bytes 393220
  0.6 2.8 %copy-start.2 = (bf16[128,1728]{0,1:T(8,128)(2,1)S(1)}, bf16[128,1728]{0,1:T(8,128)(2,1)}, u32[]{:S(2)}) copy-start(bf16[128,1728]{0,1:T(8,128)(2,1)} %param.11) | copy-start | bytes 1327108
  9.9 5.9 %copy-start.1 = (bf16[256,128,3,3,3]{0,4,3,2,1:T(4,128)(2,1)S(1)}, bf16[256,128,3,3,3]{0,4,3,2,1:T(4,128)(2,1)}, u32[]{:S(2)}) copy-start(bf16[256,128,3,3,3]{0,4,3,2,1:T(4,128)(2,1)} %reshape.52) | copy-start | bytes 5308420
  24.1 10.0 %collective-permute-start = (bf16[4,256,64]{1,2,0:T(8,128)(2,1)S(1)}, bf16[4,256,64]{1,2,0:T(8,128)(2,1)S(1)}, u32[]{:S(2)}, u32[]{:S(2)}) collective-permute-start(bf16[4,256,64]{1,2,0:T(8,128)(2,1)S(1)} %get-tuple-element.16), channel_id=1, source_target_pairs={{0,7},{1,0},{2,1},{3,2},{4,3},{5,4},{6,5},{7,6},{8,15},{9,8},{10,9... | collective-permute-start | bytes 393224 | tf_op jit(solution)/shard_map/ppermute | solution.py:126
  30.2 6.8 %collective-permute-start.1 = (bf16[4,256,64]{1,2,0:T(8,128)(2,1)S(1)}, bf16[4,256,64]{1,2,0:T(8,128)(2,1)S(1)}, u32[]{:S(2)}, u32[]{:S(2)}) collective-permute-start(bf16[4,256,64]{1,2,0:T(8,128)(2,1)S(1)} %get-tuple-element.15), channel_id=1, source_target_pairs={{0,6},{1,7},{2,0},{3,1},{4,2},{5,3},{6,4},{7,5},{8,14},{9,15},{10,... | collective-permute-start | bytes 393224 | tf_op jit(solution)/shard_map/ppermute | solution.py:126
  30.6 9.1 %collective-permute-start.2 = (bf16[4,256,64]{1,2,0:T(8,128)(2,1)S(1)}, bf16[4,256,64]{1,2,0:T(8,128)(2,1)S(1)}, u32[]{:S(2)}, u32[]{:S(2)}) collective-permute-start(bf16[4,256,64]{1,2,0:T(8,128)(2,1)S(1)} %get-tuple-element.14), channel_id=1, source_target_pairs={{0,5},{1,6},{2,7},{3,0},{4,1},{5,2},{6,3},{7,4},{8,13},{9,14},{10,... | collective-permute-start | bytes 393224 | tf_op jit(solution)/shard_map/ppermute | solution.py:126
  30.6 21.9 %collective-permute-start.3 = (bf16[4,256,64]{1,2,0:T(8,128)(2,1)S(1)}, bf16[4,256,64]{1,2,0:T(8,128)(2,1)S(1)}, u32[]{:S(2)}, u32[]{:S(2)}) collective-permute-start(bf16[4,256,64]{1,2,0:T(8,128)(2,1)S(1)} %get-tuple-element.13), channel_id=1, source_target_pairs={{0,4},{1,5},{2,6},{3,7},{4,0},{5,1},{6,2},{7,3},{8,12},{9,13},{10,... | collective-permute-start | bytes 393224 | tf_op jit(solution)/shard_map/ppermute | solution.py:126
  33.6 20.4 %collective-permute-start.4 = (bf16[4,256,64]{1,2,0:T(8,128)(2,1)S(1)}, bf16[4,256,64]{1,2,0:T(8,128)(2,1)S(1)}, u32[]{:S(2)}, u32[]{:S(2)}) collective-permute-start(bf16[4,256,64]{1,2,0:T(8,128)(2,1)S(1)} %get-tuple-element.12), channel_id=1, source_target_pairs={{0,3},{1,4},{2,5},{3,6},{4,7},{5,0},{6,1},{7,2},{8,11},{9,12},{10,... | collective-permute-start | bytes 393224 | tf_op jit(solution)/shard_map/ppermute | solution.py:126
  34.1 20.2 %copy-start.3 = (bf16[3,256,256]{2,1,0:T(8,128)(2,1)S(1)}, bf16[3,256,256]{2,1,0:T(8,128)(2,1)}, u32[]{:S(2)}) copy-start(bf16[3,256,256]{2,1,0:T(8,128)(2,1)} %param.13) | copy-start | bytes 1179652
  34.1 20.0 %collective-permute-start.5 = (bf16[4,256,64]{1,2,0:T(8,128)(2,1)S(1)}, bf16[4,256,64]{1,2,0:T(8,128)(2,1)S(1)}, u32[]{:S(2)}, u32[]{:S(2)}) collective-permute-start(bf16[4,256,64]{1,2,0:T(8,128)(2,1)S(1)} %get-tuple-element.11), channel_id=1, source_target_pairs={{0,2},{1,3},{2,4},{3,5},{4,6},{5,7},{6,0},{7,1},{8,10},{9,11},{10,... | collective-permute-start | bytes 393224 | tf_op jit(solution)/shard_map/ppermute | solution.py:126
  36.9 17.2 %collective-permute-start.6 = (bf16[4,256,64]{1,2,0:T(8,128)(2,1)S(1)}, bf16[4,256,64]{1,2,0:T(8,128)(2,1)S(1)}, u32[]{:S(2)}, u32[]{:S(2)}) collective-permute-start(bf16[4,256,64]{1,2,0:T(8,128)(2,1)S(1)} %get-tuple-element.10), channel_id=1, source_target_pairs={{0,1},{1,2},{2,3},{3,4},{4,5},{5,6},{6,7},{7,0},{8,9},{9,10},{10,1... | collective-permute-start | bytes 393224 | tf_op jit(solution)/shard_map/ppermute | solution.py:126
  57.9 3.4 %copy-start.4 = (bf16[256,256]{1,0:T(8,128)(2,1)S(1)}, bf16[256,256]{1,0:T(8,128)(2,1)}, u32[]{:S(2)}) copy-start(bf16[256,256]{1,0:T(8,128)(2,1)} %param.15) | copy-start | bytes 393220
  81.6 4.8 %copy-start.5 = (bf16[256,256]{1,0:T(8,128)(2,1)S(1)}, bf16[256,256]{1,0:T(8,128)(2,1)}, u32[]{:S(2)}) copy-start(bf16[256,256]{1,0:T(8,128)(2,1)} %param.16) | copy-start | bytes 393220
  97.5 2.2 %copy-start.6 = (bf16[256,256]{1,0:T(8,128)(2,1)S(1)}, bf16[256,256]{1,0:T(8,128)(2,1)}, u32[]{:S(2)}) copy-start(bf16[256,256]{1,0:T(8,128)(2,1)} %param.17) | copy-start | bytes 393220
